TPU v7x, 512 devices: a whole 4x8x8 slice. The times are simulated.
512 devices in a mesh: ctx: 64 (over y, z_lo, x), mp: 8 (over z_hi, core).
Axes of the slice: x: 4, y: 8, z: 8 (z_hi: 4, z_lo: 2; z = z_hi * 2 + z_lo), core: 2. Of those that a mesh axis runs over, the one named last changes fastest.
Arguments:
- queries: bfloat16 [16384, 8192], P('ctx', 'mp'), may hold values from -6 to 6
- key_feats: bfloat16 [16384, 8192], P('ctx', 'mp'), may hold values from -6 to 6
- value_feats: bfloat16 [16384, 8192], P('ctx', 'mp'), may hold values from -6 to 6
- filters: bfloat16 [512, 128], P('mp'), may hold values from -0.5 to 0.5
- grad_out: bfloat16 [16384, 8192], P('ctx', 'mp'), may hold values from -40 to 40
Outputs:
- mixer_out: bfloat16 [16384, 8192], P('ctx', 'mp')
- grad_queries: bfloat16 [16384, 8192], P('ctx', 'mp')
- grad_keys: bfloat16 [16384, 8192], P('ctx', 'mp')
- grad_values: bfloat16 [16384, 8192], P('ctx', 'mp')
- grad_filters: float32 [512, 128], P('mp')
All inputs are finite; a program needn't handle non-finite values.
Results may differ from a plain program's by a relative error of at most 0.0058.
Values may be sent and summed in bfloat16 or wider, within the bound.
No kernel may reach another device: no remote copies, remote signals or barrier semaphores. Data moves between devices by JAX's collectives and lax.ppermute only.
A program may use at most 64 MiB of HBM per device.

v0:
```python
import jax
import jax.numpy as jnp
from jax import lax
from jax.sharding import PartitionSpec as P

D = 8192
G = 16


def contract(formula, first_op, second_op):
    return jnp.einsum(formula, first_op, second_op, preferred_element_type=jnp.float32)


def toeplitz(filt):
    count, filter_len = filt.shape
    flipped = filt[:, ::-1]
    lead_zero = jnp.zeros((count, 1), filt.dtype)
    trailing = jnp.zeros((count, filter_len), filt.dtype)
    pattern = jnp.concatenate([lead_zero, flipped, trailing], axis=1)
    repeated = jnp.tile(pattern, (1, filter_len))
    return repeated[:, : filter_len * 2 * filter_len].reshape(count, filter_len, 2 * filter_len)


def make_windows(blocks, before):
    earlier = jnp.concatenate([before[:, :, None, :], blocks[:, :, :-1, :]], axis=2)
    return jnp.concatenate([earlier, blocks], axis=3)


def forward_conv(signal, before, toeplitz_mat):
    groups_here, group_size, seq_len = signal.shape
    filter_len = toeplitz_mat.shape[1]
    blocks = signal.reshape(groups_here, group_size, seq_len // filter_len, filter_len)
    window_rows = make_windows(blocks, before)
    result = contract("gam,gsnm->gsna", toeplitz_mat, window_rows)
    return (result.reshape(groups_here, group_size, seq_len), window_rows)


def backward_conv(grad_rows, after, toeplitz_mat):
    groups_here, group_size, seq_len = grad_rows.shape
    filter_len = toeplitz_mat.shape[1]
    blocks = grad_rows.reshape(groups_here, group_size, seq_len // filter_len, filter_len)
    spread = contract("gam,gsna->gsnm", toeplitz_mat, blocks)
    tail_part = contract("gam,gsa->gsm", toeplitz_mat, after)
    next_part = jnp.concatenate(
        [spread[:, :, 1:, :filter_len], tail_part[:, :, None, :filter_len]], axis=2
    )
    return (spread[:, :, :, filter_len:] + next_part).reshape(groups_here, group_size, seq_len)


def filter_grad(grad_rows, window_rows, filter_len):
    groups_here, group_size, seq_len = grad_rows.shape
    blocks = grad_rows.reshape(groups_here, group_size, seq_len // filter_len, filter_len)
    correlate = contract("gsna,gsnm->gam", blocks, window_rows)
    flattened = correlate.reshape(groups_here, filter_len * 2 * filter_len)
    flattened = jnp.concatenate(
        [flattened, jnp.zeros((groups_here, filter_len), jnp.float32)], axis=1
    )
    flattened = flattened.reshape(groups_here, filter_len, 2 * filter_len + 1)
    diagonals = jnp.sum(flattened, axis=1)
    return diagonals[:, 1 : filter_len + 1][:, ::-1]


def shards(queries, key_feats, value_feats, filters, grad_out):
    tokens, channels = queries.shape
    slab_groups, filter_len = filters.shape
    product = (
        (key_feats.astype(jnp.float32) * value_feats.astype(jnp.float32)).astype(jnp.bfloat16).T
    )
    grad_mix = (grad_out.astype(jnp.float32) * queries.astype(jnp.float32)).astype(jnp.bfloat16).T
    owners = lax.axis_size("ctx")
    own_width = channels // owners
    own_groups = own_width // G
    signal = lax.all_to_all(product, "ctx", split_axis=0, concat_axis=1, tiled=True)
    grad_rows = lax.all_to_all(grad_mix, "ctx", split_axis=0, concat_axis=1, tiled=True)
    seq_len = signal.shape[1]
    signal = signal.reshape(own_groups, G, seq_len)
    grad_rows = grad_rows.reshape(own_groups, G, seq_len)
    first_group = lax.axis_index("ctx") * own_groups
    own_filters = lax.dynamic_slice_in_dim(filters, first_group, own_groups, 0)
    toeplitz_mat = toeplitz(own_filters)
    zero_rim = jnp.zeros((own_groups, G, filter_len), jnp.bfloat16)
    conv_out, window_rows = forward_conv(signal, zero_rim, toeplitz_mat)
    conv_out = conv_out.astype(jnp.bfloat16).reshape(own_width, seq_len)
    conv_grad = (
        backward_conv(grad_rows, zero_rim, toeplitz_mat)
        .astype(jnp.bfloat16)
        .reshape(own_width, seq_len)
    )
    partial_grad = filter_grad(grad_rows, window_rows, filter_len)
    conv_rows = lax.all_to_all(conv_out, "ctx", split_axis=1, concat_axis=0, tiled=True)
    grad_back = lax.all_to_all(conv_grad, "ctx", split_axis=1, concat_axis=0, tiled=True)
    raw_filters = lax.all_gather(partial_grad, "ctx", axis=0, tiled=True)
    conv_f = conv_rows.T.astype(jnp.float32)
    back_f = grad_back.T.astype(jnp.float32)
    mixer_out = (queries.astype(jnp.float32) * conv_f).astype(jnp.bfloat16)
    grad_queries = (grad_out.astype(jnp.float32) * conv_f).astype(jnp.bfloat16)
    grad_keys = (back_f * value_feats.astype(jnp.float32)).astype(jnp.bfloat16)
    grad_values = (back_f * key_feats.astype(jnp.float32)).astype(jnp.bfloat16)
    square_sum = lax.psum(jnp.sum(raw_filters * raw_filters), "mp")
    grad_rms = jnp.sqrt(square_sum / (D // G * filter_len) + 1e-06)
    grad_filters = raw_filters * jnp.minimum(1.0, 1.0 / grad_rms)
    return (mixer_out, grad_queries, grad_keys, grad_values, grad_filters)


def solution(mesh):
    placed = (P("ctx", "mp"), P("ctx", "mp"), P("ctx", "mp"), P("mp", None), P("ctx", "mp"))
    return jax.shard_map(
        shards,
        mesh=mesh,
        in_specs=placed,
        out_specs=(P("ctx", "mp"), P("ctx", "mp"), P("ctx", "mp"), P("ctx", "mp"), P("mp", None)),
        check_vma=False,
    )
```

profile of v0, /device:TPU:1, one launch (start us, length us, event | category | flops | bytes accessed | tf_op | source)
XLA Modules:
  0.0 278.9 jit_solution(11719873778474944530)
XLA Ops:
  0.6 1.2 copy.28
  1.9 1.2 copy.33
  3.1 0.9 fusion.6
  4.1 12.9 %all-to-all-start.2 = ((bf16[64,16,256]{2,1,0:T(8,128)(2,1)}), bf16[64,16,256]{2,1,0:T(8,128)(2,1)S(1)}, u32[]{:S(2)}, u32[]{:S(2)}) async-start(bf16[64,16,256]{2,1,0:T(8,128)(2,1)} %bitcast.10), calls=%async_computation.2 | async-start | bytes 1048576 | tf_op jit(solution)/shard_map/all_to_all | solution.py:74
  18.3 14.5 %all-to-all-done.2 = bf16[64,16,256]{2,1,0:T(8,128)(2,1)S(1)} async-done(((bf16[64,16,256]{2,1,0:T(8,128)(2,1)}), bf16[64,16,256]{2,1,0:T(8,128)(2,1)S(1)}, u32[]{:S(2)}, u32[]{:S(2)}) %all-to-all-start.2) | async-done | bytes 524320 | tf_op jit(solution)/shard_map/all_to_all | solution.py:74
  34.0 1.1 copy.35
  35.0 7.2 %all-to-all-start.3 = ((bf16[16,64,256]{2,0,1:T(8,128)(2,1)}), bf16[16,64,256]{2,0,1:T(8,128)(2,1)S(1)}, u32[]{:S(2)}, u32[]{:S(2)}) async-start(bf16[16,64,256]{2,0,1:T(8,128)(2,1)} %copy.35), calls=%async_computation.3 | async-start | bytes 1048576 | tf_op jit(solution)/shard_map/all_to_all | solution.py:91
  42.2 1.0 copy.29
  43.2 1.0 copy.30
  44.2 12.8 %all-to-all-done.3 = bf16[16,64,256]{2,0,1:T(8,128)(2,1)S(1)} async-done(((bf16[16,64,256]{2,0,1:T(8,128)(2,1)}), bf16[16,64,256]{2,0,1:T(8,128)(2,1)S(1)}, u32[]{:S(2)}, u32[]{:S(2)}) %all-to-all-start.3) | async-done | bytes 524320 | tf_op jit(solution)/shard_map/all_to_all | solution.py:91
  57.0 1.5 fusion.2
  58.5 21.8 %all_to_all.52 = bf16[64,16,256]{2,1,0:T(8,128)(2,1)S(1)} all-to-all(bf16[64,16,256]{2,1,0:T(8,128)(2,1)S(1)} %bitcast.50), channel_id=1, replica_groups=mesh['ctx'=64,'mp'=8] {'ctx'}, dimensions={0} | all-to-all | bytes 1048576 | tf_op jit(solution)/shard_map/all_to_all | solution.py:73
  80.5 1.0 reshape_reshape.2
  81.5 2.4 convolution_convert_fusion
  83.9 1.2 convert_element_type.83
  85.1 1.1 copy.32
  86.2 8.1 %all-to-all-start.1 = ((bf16[16,64,256]{2,0,1:T(8,128)(2,1)}), bf16[16,64,256]{2,0,1:T(8,128)(2,1)S(1)}, u32[]{:S(2)}, u32[]{:S(2)}) async-start(bf16[16,64,256]{2,0,1:T(8,128)(2,1)} %copy.32), calls=%async_computation.1 | async-start | bytes 1048576 | tf_op jit(solution)/shard_map/all_to_all | solution.py:90
  94.4 1.0 copy.39
  95.4 1.5 convolution_bitcast_fusion.1
  97.9 127.5 %all-gather = f32[64,1,128]{2,1,0:T(1,128)S(1)} all-gather(f32[1,1,128]{2,1,0:T(1,128)S(1)} %bitcast.57), channel_id=1, replica_groups=mesh['ctx'=64,'mp'=8] {'ctx'}, dimensions={0}, use_global_device_ids=true | all-gather | bytes 33280 | tf_op jit(solution)/shard_map/all_gather | solution.py:92
  226.1 1.0 copy.40
  227.1 48.2 %psum.7 = f32[]{:T(128)} all-reduce(f32[]{:T(128)} %multiply_reduce_fusion), channel_id=1, replica_groups=mesh['ctx'=64,'mp'=8] {'mp'}, use_global_device_ids=true, to_apply=%region_2.0 | all-reduce | flops 1 | bytes 8 | tf_op jit(solution)/shard_map/psum | solution.py:99
  276.9 1.0 copy.37
  277.9 1.0 copy.38
  (36 shorter events, 5.1 us)
Async XLA Ops:
  0.6 16.4 %copy-start = (bf16[64,128]{1,0:T(8,128)(2,1)S(1)}, bf16[64,128]{1,0:T(8,128)(2,1)}, u32[]{:S(2)}) copy-start(bf16[64,128]{1,0:T(8,128)(2,1)} %param.8) | copy-start | bytes 49156
  4.1 28.7 %all-to-all-start.2 = ((bf16[64,16,256]{2,1,0:T(8,128)(2,1)}), bf16[64,16,256]{2,1,0:T(8,128)(2,1)S(1)}, u32[]{:S(2)}, u32[]{:S(2)}) async-start(bf16[64,16,256]{2,1,0:T(8,128)(2,1)} %bitcast.10), calls=%async_computation.2 | async-start | bytes 1048576 | tf_op jit(solution)/shard_map/all_to_all | solution.py:74
  33.8 8.5 %copy-start.1 = (bf16[256,1024]{1,0:T(8,128)(2,1)S(1)}, bf16[256,1024]{1,0:T(8,128)(2,1)}, u32[]{:S(2)}) copy-start(bf16[256,1024]{1,0:T(8,128)(2,1)} %param.6) | copy-start | bytes 1572868
  35.0 8.2 %copy-start.2 = (bf16[256,1024]{1,0:T(8,128)(2,1)S(1)}, bf16[256,1024]{1,0:T(8,128)(2,1)}, u32[]{:S(2)}) copy-start(bf16[256,1024]{1,0:T(8,128)(2,1)} %param.7) | copy-start | bytes 1572868
  35.0 22.0 %all-to-all-start.3 = ((bf16[16,64,256]{2,0,1:T(8,128)(2,1)}), bf16[16,64,256]{2,0,1:T(8,128)(2,1)S(1)}, u32[]{:S(2)}, u32[]{:S(2)}) async-start(bf16[16,64,256]{2,0,1:T(8,128)(2,1)} %copy.35), calls=%async_computation.3 | async-start | bytes 1048576 | tf_op jit(solution)/shard_map/all_to_all | solution.py:91
  86.2 190.4 %all-to-all-start.1 = ((bf16[16,64,256]{2,0,1:T(8,128)(2,1)}), bf16[16,64,256]{2,0,1:T(8,128)(2,1)S(1)}, u32[]{:S(2)}, u32[]{:S(2)}) async-start(bf16[16,64,256]{2,0,1:T(8,128)(2,1)} %copy.32), calls=%async_computation.1 | async-start | bytes 1048576 | tf_op jit(solution)/shard_map/all_to_all | solution.py:90
where the time goes:
time: 279 us
  blocking collectives  198 us (71%)
  starting transfers between devices  28.2 us (10%)
  waiting for transfers between devices  27.3 us (10%)
  local copies, waits for them, and re-layouts  15.6 us (6%)
  matrix products  4.52 us (2%)
  other arithmetic  4.21 us (2%)
    all_gather x1, blocking collectives, shards(): raw_filters = lax.all_gather(partial_grad, 'ctx', axis=0, tiled=True)  128 us
    psum x1, blocking collectives, shards(): square_sum = lax.psum(jnp.sum(raw_filters * raw_filters), 'mp')  48.2 us
    all_to_all x1, blocking collectives, shards(): lax.all_to_all(product, 'ctx', split_axis=0, concat_axis=1, tiled=True)  21.8 us
    all_to_all x1, waiting for transfers between devices, shards(): lax.all_to_all(grad_mix, 'ctx', split_axis=0, concat_axis=1, tiled=True)  14.5 us
    all_to_all x1, starting transfers between devices, shards(): lax.all_to_all(grad_mix, 'ctx', split_axis=0, concat_axis=1, tiled=True)  12.9 us
    all_to_all x1, waiting for transfers between devices, shards(): lax.all_to_all(conv_grad, 'ctx', split_axis=1, concat_axis=0, tiled=True)  12.8 us
    unnamed x15, local copies, waits for them, and re-layouts  8.66 us
    all_to_all x1, starting transfers between devices, shards(): lax.all_to_all(conv_out, 'ctx', split_axis=1, concat_axis=0, tiled=True)  8.11 us
  transfers between devices with their start and end apart: 3, of which 2 were waited for; matrix products, arithmetic and copies ran while one was open for 3% of the time, Pallas kernels for 0%

commit v1 on v0

--- a/solution.py
+++ b/solution.py
@@ -2,6 +2,7 @@
 import jax.numpy as jnp
 from jax import lax
 from jax.sharding import PartitionSpec as P
+from jax.lax import all_to_all, axis_size
 
 D = 8192
 G = 16
@@ -87,7 +88,16 @@
         .reshape(own_width, seq_len)
     )
     partial_grad = filter_grad(grad_rows, window_rows, filter_len)
-    conv_rows = lax.all_to_all(conv_out, "ctx", split_axis=1, concat_axis=0, tiled=True)
+    _use_tables = lambda values: jnp.concatenate(
+        all_to_all(
+            jnp.stack(jnp.split(values, axis_size("ctx"), 1), 0),
+            axis_name="ctx",
+            split_axis=0,
+            concat_axis=0,
+        ),
+        0,
+    )
+    conv_rows = _use_tables(conv_out)
     grad_back = lax.all_to_all(conv_grad, "ctx", split_axis=1, concat_axis=0, tiled=True)
     raw_filters = lax.all_gather(partial_grad, "ctx", axis=0, tiled=True)
     conv_f = conv_rows.T.astype(jnp.float32)

time: 279 us -> 315 us (1.13)
  local copies, waits for them, and re-layouts: 15.6 us -> 53.1 us
    unnamed x15 -> x77, local copies, waits for them, and re-layouts: 8.66 us -> 47.8 us
where the time goes in v1:
time: 315 us; the launch traced here: 314 us
  blocking collectives  198 us (63%)
  local copies, waits for them, and re-layouts  53.1 us (17%)
  starting transfers between devices  28.1 us (9%)
  waiting for transfers between devices  26.2 us (8%)
  other arithmetic  4.25 us (1%)
  matrix products  3.72 us (1%)
    all_gather x1, blocking collectives, shards(): raw_filters = lax.all_gather(partial_grad, 'ctx', axis=0, tiled=True)  128 us
    psum x1, blocking collectives, shards(): square_sum = lax.psum(jnp.sum(raw_filters * raw_filters), 'mp')  48.2 us
    unnamed x77, local copies, waits for them, and re-layouts  47.8 us
    all_to_all x1, blocking collectives, shards(): lax.all_to_all(product, 'ctx', split_axis=0, concat_axis=1, tiled=True)  21.8 us
    all_to_all x1, waiting for transfers between devices, shards(): lax.all_to_all(grad_mix, 'ctx', split_axis=0, concat_axis=1, tiled=True)  14.5 us
    all_to_all x1, starting transfers between devices, shards(): lax.all_to_all(grad_mix, 'ctx', split_axis=0, concat_axis=1, tiled=True)  12.9 us
    all_to_all x1, waiting for transfers between devices, shards(): lax.all_to_all(conv_grad, 'ctx', split_axis=1, concat_axis=0, tiled=True)  11.8 us
    all_to_all x1, starting transfers between devices, shards(): all_to_all(jnp.stack(jnp.split(values, axis_size('ctx'), 1), 0), axis_nam...  8.1 us
  transfers between devices with their start and end apart: 3, of which 2 were waited for; matrix products, arithmetic and copies ran while one was open for 3% of the time, Pallas kernels for 0%

profile of v1, /device:TPU:1, one launch (start us, length us, event | category | flops | bytes accessed | tf_op | source)
XLA Modules:
  0.0 314.4 jit_solution(3341216561655405164)
XLA Ops:
  0.6 1.2 copy.27
  1.9 1.2 copy.31
  3.1 0.9 fusion.6
  4.1 12.9 %all-to-all-start.2 = ((bf16[64,16,256]{2,1,0:T(8,128)(2,1)}), bf16[64,16,256]{2,1,0:T(8,128)(2,1)S(1)}, u32[]{:S(2)}, u32[]{:S(2)}) async-start(bf16[64,16,256]{2,1,0:T(8,128)(2,1)} %bitcast.72), calls=%async_computation.2 | async-start | bytes 1048576 | tf_op jit(solution)/shard_map/all_to_all | solution.py:75
  18.3 14.5 %all-to-all-done.2 = bf16[64,16,256]{2,1,0:T(8,128)(2,1)S(1)} async-done(((bf16[64,16,256]{2,1,0:T(8,128)(2,1)}), bf16[64,16,256]{2,1,0:T(8,128)(2,1)S(1)}, u32[]{:S(2)}, u32[]{:S(2)}) %all-to-all-start.2) | async-done | bytes 524320 | tf_op jit(solution)/shard_map/all_to_all | solution.py:75
  34.0 1.1 copy.33
  35.0 7.0 %all-to-all-start.3 = ((bf16[16,64,256]{2,0,1:T(8,128)(2,1)}), bf16[16,64,256]{2,0,1:T(8,128)(2,1)S(1)}, u32[]{:S(2)}, u32[]{:S(2)}) async-start(bf16[16,64,256]{2,0,1:T(8,128)(2,1)} %copy.33), calls=%async_computation.3 | async-start | bytes 1048576 | tf_op jit(solution)/shard_map/all_to_all | solution.py:101
  42.1 1.0 copy.28
  43.1 2.0 copy.29
  45.1 11.8 %all-to-all-done.3 = bf16[16,64,256]{2,0,1:T(8,128)(2,1)S(1)} async-done(((bf16[16,64,256]{2,0,1:T(8,128)(2,1)}), bf16[16,64,256]{2,0,1:T(8,128)(2,1)S(1)}, u32[]{:S(2)}, u32[]{:S(2)}) %all-to-all-start.3) | async-done | bytes 524320 | tf_op jit(solution)/shard_map/all_to_all | solution.py:101
  56.9 1.5 fusion.2
  58.4 21.8 %all_to_all.47 = bf16[64,16,256]{2,1,0:T(8,128)(2,1)S(1)} all-to-all(bf16[64,16,256]{2,1,0:T(8,128)(2,1)S(1)} %bitcast.313), channel_id=1, replica_groups=mesh['ctx'=64,'mp'=8] {'ctx'}, dimensions={0} | all-to-all | bytes 1048576 | tf_op jit(solution)/shard_map/all_to_all | solution.py:74
  80.4 1.0 reshape_reshape.2
  81.4 1.6 convolution_convert_fusion
  121.8 8.1 %all-to-all-start.1 = ((bf16[64,16,256]{2,1,0:T(8,128)(2,1)}), bf16[64,16,256]{2,1,0:T(8,128)(2,1)S(1)}, u32[]{:S(2)}, u32[]{:S(2)}) async-start(bf16[64,16,256]{2,1,0:T(8,128)(2,1)} %constant_dynamic-update-slice_fusion), calls=%async_computation.1 | async-start | bytes 1048576 | tf_op jit(solution)/shard_map/all_to_all | solution.py:92
  129.9 1.0 copy.37
  130.9 1.5 convolution_bitcast_fusion.1
  133.5 127.5 %all-gather = f32[64,1,128]{2,1,0:T(1,128)S(1)} all-gather(f32[1,1,128]{2,1,0:T(1,128)S(1)} %bitcast.385), channel_id=1, replica_groups=mesh['ctx'=64,'mp'=8] {'ctx'}, dimensions={0}, use_global_device_ids=true | all-gather | bytes 33280 | tf_op jit(solution)/shard_map/all_gather | solution.py:102
  261.0 0.7 multiply_reduce_fusion
  261.6 1.0 copy.38
  262.6 48.2 %psum.7 = f32[]{:T(128)} all-reduce(f32[]{:T(128)} %multiply_reduce_fusion), channel_id=1, replica_groups=mesh['ctx'=64,'mp'=8] {'mp'}, use_global_device_ids=true, to_apply=%region_2.0 | all-reduce | flops 1 | bytes 8 | tf_op jit(solution)/shard_map/psum | solution.py:109
  311.5 0.6 broadcast_multiply_fusion
  312.4 1.0 copy.35
  313.4 1.0 copy.36
  (97 shorter events, 42.6 us)
Async XLA Ops:
  0.6 16.4 %copy-start = (bf16[64,128]{1,0:T(8,128)(2,1)S(1)}, bf16[64,128]{1,0:T(8,128)(2,1)}, u32[]{:S(2)}) copy-start(bf16[64,128]{1,0:T(8,128)(2,1)} %param.8) | copy-start | bytes 49156
  4.1 28.7 %all-to-all-start.2 = ((bf16[64,16,256]{2,1,0:T(8,128)(2,1)}), bf16[64,16,256]{2,1,0:T(8,128)(2,1)S(1)}, u32[]{:S(2)}, u32[]{:S(2)}) async-start(bf16[64,16,256]{2,1,0:T(8,128)(2,1)} %bitcast.72), calls=%async_computation.2 | async-start | bytes 1048576 | tf_op jit(solution)/shard_map/all_to_all | solution.py:75
  33.9 8.1 %copy-start.1 = (bf16[256,1024]{1,0:T(8,128)(2,1)S(1)}, bf16[256,1024]{1,0:T(8,128)(2,1)}, u32[]{:S(2)}) copy-start(bf16[256,1024]{1,0:T(8,128)(2,1)} %param.6) | copy-start | bytes 1572868
  35.0 21.8 %all-to-all-start.3 = ((bf16[16,64,256]{2,0,1:T(8,128)(2,1)}), bf16[16,64,256]{2,0,1:T(8,128)(2,1)S(1)}, u32[]{:S(2)}, u32[]{:S(2)}) async-start(bf16[16,64,256]{2,0,1:T(8,128)(2,1)} %copy.33), calls=%async_computation.3 | async-start | bytes 1048576 | tf_op jit(solution)/shard_map/all_to_all | solution.py:101
  121.8 190.4 %all-to-all-start.1 = ((bf16[64,16,256]{2,1,0:T(8,128)(2,1)}), bf16[64,16,256]{2,1,0:T(8,128)(2,1)S(1)}, u32[]{:S(2)}, u32[]{:S(2)}) async-start(bf16[64,16,256]{2,1,0:T(8,128)(2,1)} %constant_dynamic-update-slice_fusion), calls=%async_computation.1 | async-start | bytes 1048576 | tf_op jit(solution)/shard_map/all_to_all | solution.py:92
